TPU v7x, 256 devices: a whole 4x4x8 slice. The times are simulated.
256 devices in a mesh: row: 32 (over x, y, core), col: 8 (over z).
Axes of the slice: x: 4, y: 4, z: 8, core: 2. Of those that a mesh axis runs over, the one named last changes fastest.
Arguments:
- tile_values: bfloat16 [24576, 256, 256], P(('row', 'col')), may hold values from -0.375 to 0.375
- tile_coords: int32 [24576, 2], P(('row', 'col')), may hold values from 0 to 15, as said below
- live_counts: int32 [256], P(('row', 'col')), may hold values from 24 to 96, as said below
Outputs:
- range_basis: float32 [131072, 192], P(('row', 'col'))
- projected: float32 [8, 4096, 192], P('col', 'row')
Inputs may be any that keep to these rules, and one draw needn't show every extreme that they name: `tile_coords`: for each device, column 0 is below 16, column 1 is below 16, and the 96 positions of its slots are distinct. `live_counts`: some device has all 96 slots live.
All inputs are finite; a program needn't handle non-finite values.
Results may differ from a plain program's by a relative error of at most 0.0003.
Values sent between devices are 32-bit elements; how exact they have to be, the bound alone decides.
No kernel may reach another device: no remote copies, remote signals or barrier semaphores. Data moves between devices by JAX's collectives and lax.ppermute only.
A program may use at most 128 MiB of HBM per device.

v0:
```python
import math
import jax
import jax.numpy as jnp
from jax import lax
from jax.sharding import PartitionSpec as P

TB = 256
K = 192
RT = 16
CT = 16


def sketch_signs(column_ids, rank_cols):
    rank_index = jnp.arange(rank_cols, dtype=jnp.int32)
    hashed = column_ids[..., None] * rank_cols + rank_index
    hashed = hashed * 747796405 + 1442695040
    hashed = hashed ^ hashed >> 15
    hashed = hashed * 1103515245 + 12345
    hashed = hashed ^ hashed >> 13
    return (1 - 2 * (hashed >> 9 & 1)).astype(jnp.float32)


def basis_from(sketch_rows, gram_matrix, basis_scale):
    factor = jnp.linalg.cholesky(gram_matrix)
    solved = jax.scipy.linalg.solve_triangular(factor, sketch_rows.T, lower=True)
    return basis_scale * solved.T


def per_device(tile_values, tile_coords, live_counts):
    slot_count = tile_values.shape[0]
    col_index = lax.axis_index("col")
    tile_row = tile_coords[:, 0]
    tile_col = tile_coords[:, 1]
    live_mask = (jnp.arange(slot_count, dtype=jnp.int32) < live_counts[0]).astype(jnp.float32)[
        :, None, None
    ]
    column_ids = (
        col_index * (CT * TB) + tile_col[:, None] * TB + jnp.arange(TB, dtype=jnp.int32)[None, :]
    )
    test_signs = sketch_signs(column_ids, K).astype(jnp.bfloat16)
    sketch_terms = (
        jnp.einsum("tij,tjk->tik", tile_values, test_signs, preferred_element_type=jnp.float32)
        * live_mask
    )
    sketch_part = jax.ops.segment_sum(sketch_terms, tile_row, num_segments=RT).reshape(RT * TB, K)
    basis_scale = math.sqrt(RT * TB * lax.axis_size("row"))
    sketch_full = lax.psum(sketch_part, "col")
    gram_local = jnp.dot(
        sketch_full.T,
        sketch_full,
        precision=lax.Precision.HIGHEST,
        preferred_element_type=jnp.float32,
    )
    gram_matrix = lax.psum(gram_local, "row")
    basis_full = basis_from(sketch_full, gram_matrix, basis_scale)
    share_rows = RT * TB // lax.axis_size("col")
    range_basis = lax.dynamic_slice_in_dim(basis_full, col_index * share_rows, share_rows, 0)
    picked = basis_full.reshape(RT, TB, K)[tile_row]
    adjoint_terms = (
        jnp.einsum(
            "tij,tik->tjk",
            tile_values,
            picked,
            precision=lax.Precision.HIGHEST,
            preferred_element_type=jnp.float32,
        )
        * live_mask
    )
    adjoint_part = jax.ops.segment_sum(adjoint_terms, tile_col, num_segments=CT).reshape(CT * TB, K)
    projected = lax.psum_scatter(adjoint_part, "row", scatter_dimension=0, tiled=True)
    return (range_basis, projected[None])


def solution(mesh):
    in_specs = (P(("row", "col"), None, None), P(("row", "col"), None), P(("row", "col")))
    out_specs = (P(("row", "col"), None), P("col", "row", None))
    return jax.shard_map(
        per_device, mesh=mesh, in_specs=in_specs, out_specs=out_specs, check_vma=False
    )
```

profile of v0, /device:TPU:2, one launch (start us, length us, event | category | flops | bytes accessed | tf_op | source)
XLA Modules:
  0.0 484.5 jit_solution(14673898791970698551)
XLA Ops:
  7.2 0.0 all-reduce.6.cloned.1.call-start
  7.2 0.8 fusion.31
  8.0 0.1 add_multiply_fusion
  8.7 16.9 %multiply_bitcast_fusion.1 = f32[96,256,192]{1,2,0:T(8,128)} fusion(f32[96]{0:T(128)S(1)} %compare_convert_fusion, bf16[96,256,256]{2,1,0:T(8,128)(2,1)} %param.3, s32[96,256]{1,0:T(8,128)S(1)} %add_multiply_fusion), kind=kOutput, calls=%fused_computation.14 | convolution fusion | flops 2491416576 | bytes 31555968 | tf_op jit(solution)/shard_map/tij,tjk->tik/dot_general | solution.py:42
  25.6 0.3 broadcast.151.clone
  25.9 29.1 %scatter_fusion = f32[16,256,192]{1,2,0:T(8,128)S(1)} fusion(f32[16,256,192]{1,2,0:T(8,128)S(1)} %broadcast.151.clone, s32[96]{0:T(128)S(1)} %get-tuple-element.29, f32[96,256,192]{1,2,0:T(8,128)} %multiply_bitcast_fusion.1), kind=kCustom, calls=%fused_computation.1 | custom fusion | flops 4718592 | bytes 56623488 | tf_op jit(solution)/shard_map/scatter-add | solution.py:45
  55.1 2.1 copy.14
  57.1 0.0 all-reduce.6.cloned.1.call-update
  57.2 0.0 all-reduce.8.cloned.1.call-start
  57.3 94.5 %all-reduce.6.cloned.1.call-done = f32[4096,192]{0,1:T(8,128)} async-done(((f32[4096,192]{0,1:T(8,128)}), f32[4096,192]{0,1:T(8,128)}) %all-reduce.6.cloned.1.call-update) | async-done | bytes 3145744 | tf_op jit(solution)/shard_map/psum | solution.py:47
  151.7 6.2 %fusion.41 = f32[192,192]{0,1:T(8,128)} fusion(f32[4096,192]{0,1:T(8,128)} %all-reduce.6.cloned.1.call-done), kind=kOutput, calls=%fused_computation.78 | convolution fusion | flops 1811939328 | bytes 3293184 | tf_op jit(solution)/shard_map/dot_general | solution.py:48
  157.9 0.0 all-reduce.8.cloned.1.call-update
  157.9 0.2 reduce-scatter.2.cloned.1.call-start
  158.2 109.3 %all-reduce.8.cloned.1.call-done = f32[192,192]{0,1:T(8,128)} async-done(((f32[192,192]{0,1:T(8,128)}), f32[192,192]{0,1:T(8,128)}) %all-reduce.8.cloned.1.call-update) | async-done | bytes 147472 | tf_op jit(solution)/shard_map/psum | solution.py:54
  267.5 1.0 copy.9
  268.6 1.0 fusion.24
  269.5 11.7 %cholesky.51 = f32[128,128]{1,0:T(8,128)S(1)} custom-call(f32[128,128]{1,0:T(8,128)S(1)} %cholesky.124), custom_call_target="Cholesky" | custom-call | tf_op jit(solution)/shard_map/jit(cholesky)/cholesky | solution.py:24
  281.3 9.8 %custom-call.15 = f32[1,128,128]{1,2,0:T(8,128)S(1)} custom-call(f32[1,128,128]{2,1,0:T(8,128)S(1)} %get-tuple-element.23), custom_call_target="InvertDiagBlocksLowerTriangular" | custom-call | tf_op jit(solution)/shard_map/jit(cholesky)/cholesky | solution.py:24
  291.1 0.2 constant_dynamic-update-slice_fusion.1
  291.3 0.2 convolution_subtract_fusion.1
  291.5 5.8 %cholesky.110 = f32[64,64]{1,0:T(8,128)S(1)} custom-call(f32[64,64]{1,0:T(8,128)S(1)} %convolution_subtract_fusion.1), custom_call_target="Cholesky" | custom-call | tf_op jit(solution)/shard_map/jit(cholesky)/cholesky | solution.py:24
  297.4 0.6 compare_reduce_fusion
  298.0 0.6 compare_reduce_fusion.1
  300.0 0.1 fusion.25
  300.1 19.9 %custom-call.16 = f32[2,128,128]{1,2,0:T(8,128)S(1)} custom-call(f32[2,128,128]{2,1,0:T(8,128)S(1)} %pad_maximum_fusion), custom_call_target="InvertDiagBlocksLowerTriangular" | custom-call | tf_op jit(solution)/shard_map/jit(_solve_triangular)/triangular_solve | solution.py:25
  320.0 3.5 fusion.22
  323.5 2.4 convolution_subtract_fusion
  326.0 1.0 fusion.29
  327.0 0.4 maximum_multiply_fusion
  327.4 0.0 copy-start
  327.4 1.6 copy-done
  329.0 0.3 copy.17
  329.4 8.2 %gather_fusion = f32[96,256,192]{1,2,0:T(8,128)} fusion(f32[16,256,192]{1,2,0:T(8,128)S(1)} %bitcast.57, s32[1024]{0:T(1024)S(1)} %pad_clamp_fusion), kind=kCustom, calls=%fused_computation | custom fusion | bytes 37749120 | tf_op jit(solution)/shard_map/gather | solution.py:58
  337.6 21.8 %multiply_bitcast_fusion = f32[96,256,192]{1,2,0:T(8,128)} fusion(f32[96]{0:T(128)S(1)} %compare_convert_fusion, f32[96,256,192]{1,2,0:T(8,128)} %gather_fusion, bf16[96,256,256]{2,1,0:T(8,128)(2,1)} %param.3), kind=kOutput, calls=%fused_computation.13 | convolution fusion | flops 14500233216 | bytes 50332032 | tf_op jit(solution)/shard_map/tij,tik->tjk/dot_general | solution.py:60
  359.4 0.3 broadcast.151
  359.7 29.1 %scatter_fusion.1 = f32[16,256,192]{1,2,0:T(8,128)S(1)} fusion(f32[16,256,192]{1,2,0:T(8,128)S(1)} %broadcast.151, s32[96]{0:T(128)S(1)} %get-tuple-element.27, f32[96,256,192]{1,2,0:T(8,128)} %multiply_bitcast_fusion), kind=kCustom, calls=%fused_computation.2 | custom fusion | flops 4718592 | bytes 56623488 | tf_op jit(solution)/shard_map/scatter-add | solution.py:69
  388.8 2.1 copy.15
  390.9 0.0 reduce-scatter.2.cloned.1.call-update
  390.9 1.8 dynamic-slice_bitcast_fusion
  392.7 85.3 %reduce-scatter.2.cloned.1.call-done = f32[128,192]{0,1:T(8,128)} async-done(((f32[4096,192]{0,1:T(8,128)}), f32[128,192]{0,1:T(8,128)}) %reduce-scatter.2.cloned.1.call-update) | async-done | bytes 98320 | tf_op jit(solution)/shard_map/reduce_scatter | solution.py:70
  (11 shorter events, 0.2 us)
Async XLA Ops:
  7.2 144.6 %all-reduce.6.cloned.1.call-start = ((), (), s32[]{:S(2)}) async-start(), calls=%async_computation.1 | async-start | bytes 6291456 | tf_op jit(solution)/shard_map/psum | solution.py:47
  57.2 210.3 %all-reduce.8.cloned.1.call-start = ((), (), s32[]{:S(2)}) async-start(), calls=%async_computation.2 | async-start | bytes 393216 | tf_op jit(solution)/shard_map/psum | solution.py:54
  157.9 320.0 %reduce-scatter.2.cloned.1.call-start = ((), (), s32[]{:S(2)}) async-start(), calls=%async_computation.3 | async-start | bytes 3244032 | tf_op jit(solution)/shard_map/reduce_scatter | solution.py:70
  327.4 1.6 copy-start
Sparse Core Ops, SparseCore 0:
  57.3 94.3 all-reduce.5
  158.1 109.3 all-reduce.7
  391.0 86.8 reduce-scatter.1
where the time goes:
time: 485 us; the launch traced here: 484 us
  waiting for transfers between devices  289 us (60%)
  other arithmetic  109 us (22%)
  matrix products  52.2 us (11%)
  local copies, waits for them, and re-layouts  17.8 us (4%)
  between operations  15.9 us (3%)
    psum x1, waiting for transfers between devices, per_device(): gram_matrix = lax.psum(gram_local, 'row')  109 us
    psum x1, waiting for transfers between devices, per_device(): sketch_full = lax.psum(sketch_part, 'col')  94.5 us
    reduce_scatter x1, waiting for transfers between devices, per_device(): lax.psum_scatter(adjoint_part, 'row', scatter_dimension=0, tiled=True)  85.3 us
    scatter-add x1, other arithmetic, per_device(): jax.ops.segment_sum(sketch_terms, tile_row, num_segments=RT)  29.1 us
    scatter-add x1, other arithmetic, per_device(): jax.ops.segment_sum(adjoint_terms, tile_col, num_segments=CT)  29.1 us
    another operation x7, other arithmetic, basis_from(): factor = jnp.linalg.cholesky(gram_matrix)  28.7 us
    dot_general x1, matrix products, per_device(): jnp.einsum('tij,tik->tjk', tile_values, picked, precision=lax.Precision.H...  21.8 us
    another operation x6, other arithmetic, basis_from(): jax.scipy.linalg.solve_triangular(factor, sketch_rows.T, lower=True)  20 us
  transfers between devices with their start and end apart: 3, of which 3 were waited for; matrix products, arithmetic and copies ran while one was open for 0% of the time, Pallas kernels for 0%

commit v1 on v0

--- a/solution.py
+++ b/solution.py
@@ -51,7 +51,7 @@
         precision=lax.Precision.HIGHEST,
         preferred_element_type=jnp.float32,
     )
-    gram_matrix = lax.psum(gram_local, "row")
+    gram_matrix = jnp.sum(lax.all_gather(gram_local, "row"), axis=0)
     basis_full = basis_from(sketch_full, gram_matrix, basis_scale)
     share_rows = RT * TB // lax.axis_size("col")
     range_basis = lax.dynamic_slice_in_dim(basis_full, col_index * share_rows, share_rows, 0)

time: 485 us -> 430 us (0.89)
  waiting for transfers between devices: 289 us -> 232 us
    psum x1 -> x0, waiting for transfers between devices: 109 us -> none  [per_device(): gram_matrix = lax.psum(gram_local, 'row')]
    all_gather x0 -> x1, waiting for transfers between devices: none -> 51.6 us  [per_device(): gram_matrix = jnp.sum(lax.all_gather(gram_local, 'row'), axis=0)]
where the time goes in v1:
time: 430 us; the launch traced here: 429 us
  waiting for transfers between devices  232 us (54%)
  other arithmetic  112 us (26%)
  matrix products  52.2 us (12%)
  local copies, waits for them, and re-layouts  16.8 us (4%)
  between operations  15.9 us (4%)
    psum x1, waiting for transfers between devices, per_device(): sketch_full = lax.psum(sketch_part, 'col')  94.5 us
    reduce_scatter x1, waiting for transfers between devices, per_device(): lax.psum_scatter(adjoint_part, 'row', scatter_dimension=0, tiled=True)  86 us
    all_gather x1, waiting for transfers between devices, per_device(): gram_matrix = jnp.sum(lax.all_gather(gram_local, 'row'), axis=0)  51.6 us
    scatter-add x1, other arithmetic, per_device(): jax.ops.segment_sum(sketch_terms, tile_row, num_segments=RT)  29.1 us
    scatter-add x1, other arithmetic, per_device(): jax.ops.segment_sum(adjoint_terms, tile_col, num_segments=CT)  29.1 us
    another operation x7, other arithmetic, basis_from(): factor = jnp.linalg.cholesky(gram_matrix)  28.7 us
    dot_general x1, matrix products, per_device(): jnp.einsum('tij,tik->tjk', tile_values, picked, precision=lax.Precision.H...  21.8 us
    another operation x6, other arithmetic, basis_from(): jax.scipy.linalg.solve_triangular(factor, sketch_rows.T, lower=True)  20 us
  transfers between devices with their start and end apart: 3, of which 3 were waited for; matrix products, arithmetic and copies ran while one was open for 0% of the time, Pallas kernels for 0%

profile of v1, /device:TPU:2, one launch (start us, length us, event | category | flops | bytes accessed | tf_op | source)
XLA Modules:
  0.0 428.9 jit_solution(9393843015666300661)
XLA Ops:
  7.2 0.0 all-reduce.5.cloned.1.call-start
  7.2 0.8 fusion.31
  8.0 0.1 add_multiply_fusion
  8.7 16.9 %multiply_bitcast_fusion.1 = f32[96,256,192]{1,2,0:T(8,128)} fusion(f32[96]{0:T(128)S(1)} %compare_convert_fusion, bf16[96,256,256]{2,1,0:T(8,128)(2,1)} %param.3, s32[96,256]{1,0:T(8,128)S(1)} %add_multiply_fusion), kind=kOutput, calls=%fused_computation.14 | convolution fusion | flops 2491416576 | bytes 31555968 | tf_op jit(solution)/shard_map/tij,tjk->tik/dot_general | solution.py:42
  25.6 0.3 broadcast.151.clone
  25.9 29.1 %scatter_fusion = f32[16,256,192]{1,2,0:T(8,128)S(1)} fusion(f32[16,256,192]{1,2,0:T(8,128)S(1)} %broadcast.151.clone, s32[96]{0:T(128)S(1)} %get-tuple-element.29, f32[96,256,192]{1,2,0:T(8,128)} %multiply_bitcast_fusion.1), kind=kCustom, calls=%fused_computation.1 | custom fusion | flops 4718592 | bytes 56623488 | tf_op jit(solution)/shard_map/scatter-add | solution.py:45
  55.1 2.1 copy.15
  57.1 0.0 all-reduce.5.cloned.1.call-update
  57.1 0.0 all-gather.3.cloned.1.call-start
  57.2 94.5 %all-reduce.5.cloned.1.call-done = f32[4096,192]{0,1:T(8,128)} async-done(((f32[4096,192]{0,1:T(8,128)}), f32[4096,192]{0,1:T(8,128)}) %all-reduce.5.cloned.1.call-update) | async-done | bytes 3145744 | tf_op jit(solution)/shard_map/psum | solution.py:47
  151.7 6.2 %fusion.41 = f32[192,192]{1,0:T(8,128)} fusion(f32[4096,192]{0,1:T(8,128)} %all-reduce.5.cloned.1.call-done), kind=kOutput, calls=%fused_computation.78 | convolution fusion | flops 1811939328 | bytes 3293184 | tf_op jit(solution)/shard_map/dot_general | solution.py:48
  157.9 0.0 all-gather.3.cloned.1.call-update
  157.9 0.2 reduce-scatter.2.cloned.1.call-start
  158.2 51.6 %all-gather.3.cloned.1.call-done = f32[6144,192]{1,0:T(8,128)} async-done(((f32[192,192]{1,0:T(8,128)}), f32[6144,192]{1,0:T(8,128)}) %all-gather.3.cloned.1.call-update) | async-done | bytes 4718608 | tf_op jit(solution)/shard_map/all_gather | solution.py:54
  209.7 3.2 reduce_sum.9
  213.0 0.1 copy.11
  213.2 11.7 %cholesky.51 = f32[128,128]{1,0:T(8,128)S(1)} custom-call(f32[128,128]{1,0:T(8,128)S(1)} %cholesky.124), custom_call_target="Cholesky" | custom-call | tf_op jit(solution)/shard_map/jit(cholesky)/cholesky | solution.py:24
  224.9 9.8 %custom-call.15 = f32[1,128,128]{1,2,0:T(8,128)S(1)} custom-call(f32[1,128,128]{2,1,0:T(8,128)S(1)} %get-tuple-element.23), custom_call_target="InvertDiagBlocksLowerTriangular" | custom-call | tf_op jit(solution)/shard_map/jit(cholesky)/cholesky | solution.py:24
  234.7 0.2 constant_dynamic-update-slice_fusion.1
  234.9 0.2 convolution_subtract_fusion.1
  235.1 5.8 %cholesky.110 = f32[64,64]{1,0:T(8,128)S(1)} custom-call(f32[64,64]{1,0:T(8,128)S(1)} %convolution_subtract_fusion.1), custom_call_target="Cholesky" | custom-call | tf_op jit(solution)/shard_map/jit(cholesky)/cholesky | solution.py:24
  241.0 0.6 compare_reduce_fusion
  241.6 0.6 compare_reduce_fusion.1
  243.6 0.1 fusion.25
  243.7 19.9 %custom-call.16 = f32[2,128,128]{1,2,0:T(8,128)S(1)} custom-call(f32[2,128,128]{2,1,0:T(8,128)S(1)} %pad_maximum_fusion), custom_call_target="InvertDiagBlocksLowerTriangular" | custom-call | tf_op jit(solution)/shard_map/jit(_solve_triangular)/triangular_solve | solution.py:25
  263.6 3.5 fusion.22
  267.1 2.4 convolution_subtract_fusion
  269.6 1.0 fusion.29
  270.6 0.4 maximum_multiply_fusion
  271.0 0.0 copy-start
  271.0 1.6 copy-done
  272.6 0.3 copy.18
  273.0 8.2 %gather_fusion = f32[96,256,192]{1,2,0:T(8,128)} fusion(f32[16,256,192]{1,2,0:T(8,128)S(1)} %bitcast.58, s32[1024]{0:T(1024)S(1)} %pad_clamp_fusion), kind=kCustom, calls=%fused_computation | custom fusion | bytes 37749120 | tf_op jit(solution)/shard_map/gather | solution.py:58
  281.2 21.8 %multiply_bitcast_fusion = f32[96,256,192]{1,2,0:T(8,128)} fusion(f32[96]{0:T(128)S(1)} %compare_convert_fusion, f32[96,256,192]{1,2,0:T(8,128)} %gather_fusion, bf16[96,256,256]{2,1,0:T(8,128)(2,1)} %param.3), kind=kOutput, calls=%fused_computation.13 | convolution fusion | flops 14500233216 | bytes 50332032 | tf_op jit(solution)/shard_map/tij,tik->tjk/dot_general | solution.py:60
  303.0 0.3 broadcast.151
  303.3 29.1 %scatter_fusion.1 = f32[16,256,192]{1,2,0:T(8,128)S(1)} fusion(f32[16,256,192]{1,2,0:T(8,128)S(1)} %broadcast.151, s32[96]{0:T(128)S(1)} %get-tuple-element.27, f32[96,256,192]{1,2,0:T(8,128)} %multiply_bitcast_fusion), kind=kCustom, calls=%fused_computation.2 | custom fusion | flops 4718592 | bytes 56623488 | tf_op jit(solution)/shard_map/scatter-add | solution.py:69
  332.4 2.1 copy.16
  334.5 0.0 reduce-scatter.2.cloned.1.call-update
  334.5 1.8 dynamic-slice_bitcast_fusion
  336.3 86.0 %reduce-scatter.2.cloned.1.call-done = f32[128,192]{0,1:T(8,128)} async-done(((f32[4096,192]{0,1:T(8,128)}), f32[128,192]{0,1:T(8,128)}) %reduce-scatter.2.cloned.1.call-update) | async-done | bytes 98320 | tf_op jit(solution)/shard_map/reduce_scatter | solution.py:70
  (12 shorter events, 0.2 us)
Async XLA Ops:
  7.2 144.5 %all-reduce.5.cloned.1.call-start = ((), (), s32[]{:S(2)}) async-start(), calls=%async_computation.1 | async-start | bytes 6291456 | tf_op jit(solution)/shard_map/psum | solution.py:47
  57.1 152.6 %all-gather.3.cloned.1.call-start = ((), (), s32[]{:S(2)}) async-start(), calls=%async_computation.3 | async-start | bytes 6488064 | tf_op jit(solution)/shard_map/all_gather | solution.py:54
  157.9 264.4 %reduce-scatter.2.cloned.1.call-start = ((), (), s32[]{:S(2)}) async-start(), calls=%async_computation.2 | async-start | bytes 3244032 | tf_op jit(solution)/shard_map/reduce_scatter | solution.py:70
  271.0 1.6 copy-start
Sparse Core Ops, SparseCore 0:
  57.3 94.3 all-reduce.4
  158.0 51.6 all-gather.2
  334.6 87.6 reduce-scatter.1
